TPU v7x, 32 devices: a whole 2x2x4 slice. The times are simulated.
32 devices in a mesh: groups: 2 (over y), dp: 4 (over z), net: 4 (over x, core).
Axes of the slice: x: 2, y: 2, z: 4, core: 2. Of those that a mesh axis runs over, the one named last changes fastest.
Arguments:
- part_emb: bfloat16 [8192, 512], P(('groups', 'dp', 'net')), parts along dimension 0, may hold values from -6 to 6
- assign: int32 [8192], P(('groups', 'dp', 'net')), parts along dimension 0, may hold values from 0 to 2047, as said below
- images: bfloat16 [4096, 512], P(('groups', 'dp', 'net')), parts along dimension 0, may hold values from -6 to 6
- negatives: int32 [32, 16], P('groups'), parts along dimension 0, may hold values from 0 to 1, as said below
Outputs:
- pair_loss: float32 [4096], P(('groups', 'dp', 'net')), parts along dimension 0
- net_grad: float32 [4096, 512], P(('groups', 'dp', 'net')), parts along dimension 0
- image_grad: float32 [4096, 512], P(('groups', 'dp', 'net')), parts along dimension 0
There are 2 independent parts, one for each index of `groups`. A program takes and returns all parts, laid end to end along the dimension named above; each array names one. Nothing has to cross between parts.
Inputs may be any that keep to these rules, and one draw needn't show every extreme that they name: Partition i belongs to a pair of its own run: assign[i] // 512 == i // 1024; every pair has one partition or more. An entry 1 marks a column block used as hard negatives of a row block; counts differ widely between row blocks; every row block marks at least one column block of another run; the diagonal block is used whatever its entry.
All inputs are finite; a program needn't handle non-finite values.
Results may differ from a plain program's by a relative error of at most 0.005.
Values may be sent and summed in bfloat16 or wider, within the bound.
A program may use at most 64 MiB of HBM per device.

v0:
```python
import jax
import jax.numpy as jnp
from jax import lax
from jax.sharding import PartitionSpec as P

BLOCK = 128


logit_scale = 10.0


def passed_along(block, axis, distance):
    devices = range(lax.axis_size(axis))
    route = [((i - distance) % len(devices), i) for i in devices]
    return lax.ppermute(block, axis, route)


def unit_rows(matrix):
    squares = jnp.sum(matrix * matrix, axis=1, keepdims=True)
    return (matrix * lax.rsqrt(squares + 1e-06)).astype(jnp.bfloat16)


def pass_on(accum_grad):
    return passed_along(accum_grad, "dp", 1)


def per_device(part_emb, assign, images, negatives):
    rows_dev = images.shape[0]
    emb_width = images.shape[1]
    net_size = lax.axis_size("net")
    dp_size = lax.axis_size("dp")
    net_index = lax.axis_index("net")
    dp_index = lax.axis_index("dp")
    pair_dp = rows_dev * net_size
    row_blocks = pair_dp // BLOCK
    own_blocks = rows_dev // BLOCK
    local_pairs = assign - dp_index * pair_dp
    member = local_pairs[None, :] == jnp.arange(pair_dp, dtype=jnp.int32)[:, None]
    partial_sums = jnp.dot(
        member.astype(jnp.bfloat16), part_emb, preferred_element_type=jnp.float32
    )
    pair_counts = jnp.sum(member.astype(jnp.float32), axis=1)
    pooled_sums, pooled_counts = (
        lax.psum_scatter(partial_sums, "net", scatter_dimension=0, tiled=True),
        lax.psum_scatter(pair_counts, "net", scatter_dimension=0, tiled=True),
    )
    unit_all = lax.all_gather(
        unit_rows(pooled_sums / pooled_counts[:, None]), "net", axis=0, tiled=True
    )
    unit_own = lax.dynamic_slice_in_dim(unit_all, net_index * rows_dev, rows_dev, 0)
    image_unit = unit_rows(images.astype(jnp.float32))
    row_slab = lax.dynamic_slice_in_dim(negatives, dp_index * row_blocks, row_blocks, 0)
    row_slab = row_slab.reshape(row_blocks, dp_size, net_size, own_blocks)
    column_pick = lax.dynamic_slice_in_dim(row_slab, net_index, 1, 2).reshape(
        row_blocks, dp_size * own_blocks
    )
    row_ids = dp_index * row_blocks + jnp.arange(row_blocks, dtype=jnp.int32)[:, None]
    column_pos = jnp.arange(dp_size * own_blocks, dtype=jnp.int32)[None, :]
    column_ids = (
        column_pos // own_blocks * net_size + net_index
    ) * own_blocks + column_pos % own_blocks
    diagonal = (row_ids == column_ids).astype(jnp.int32)
    live_blocks = jnp.maximum(column_pick, diagonal).astype(jnp.float32)

    def masked_exp(shard_rows, block_mask):
        col_blocks = shard_rows.shape[0] // BLOCK
        logits = logit_scale * jnp.einsum(
            "re,ce->rc", unit_all, shard_rows, preferred_element_type=jnp.float32
        )
        weights = jnp.exp(logits).reshape(row_blocks, BLOCK, col_blocks, BLOCK)
        weights = weights * block_mask[:, None, :, None]
        return weights.reshape(pair_dp, col_blocks * BLOCK)

    start_totals = jnp.zeros((pair_dp,), jnp.float32)
    shard_rows = lax.all_gather(image_unit, "dp", axis=0, tiled=True)
    col_blocks = shard_rows.shape[0] // BLOCK
    block_mask = live_blocks

    def add_compute_block(current):
        return jnp.sum(masked_exp(shard_rows, block_mask), axis=1)

    partial_totals = lax.cond(
        jnp.any(block_mask > 0), add_compute_block, lambda current: current, start_totals
    )
    row_totals = lax.psum(partial_totals, "net")

    def contribute(shard_rows, block_mask, grad_rows):
        soft_weights = (masked_exp(shard_rows, block_mask) / row_totals[:, None]).astype(
            jnp.bfloat16
        )
        grad_rows = grad_rows + logit_scale * jnp.dot(
            soft_weights, shard_rows, preferred_element_type=jnp.float32
        )
        column_grad = logit_scale * jnp.einsum(
            "rc,re->ce", soft_weights, unit_all, preferred_element_type=jnp.float32
        )
        return (grad_rows, column_grad)

    zero_rows = jnp.zeros((pair_dp, emb_width), jnp.float32)

    def visit(shard_rows, source, accum_grad, grad_rows):
        block_mask = lax.dynamic_slice_in_dim(live_blocks, source * own_blocks, own_blocks, 1)

        def visit_compute_block(operands):
            new_rows, column_grad = contribute(shard_rows, block_mask, operands[1])
            return (operands[0] + column_grad, new_rows)

        return lax.cond(
            jnp.any(block_mask > 0),
            visit_compute_block,
            lambda operands: operands,
            (accum_grad, grad_rows),
        )

    def cycle_turn(turn_index, cycle_state):
        shard_rows, accum_grad, grad_rows = cycle_state
        next_rows = passed_along(shard_rows, "dp", 1)
        source = (dp_index - turn_index) % dp_size
        accum_grad, grad_rows = visit(shard_rows, source, accum_grad, grad_rows)
        return (next_rows, pass_on(accum_grad), grad_rows)

    start_state = (image_unit, jnp.zeros((rows_dev, emb_width), jnp.float32), zero_rows)
    shard_rows, accum_grad, grad_rows = lax.fori_loop(0, dp_size - 1, cycle_turn, start_state)
    accum_grad, grad_rows = visit(shard_rows, (dp_index + 1) % dp_size, accum_grad, grad_rows)
    column_total = pass_on(accum_grad)
    row_total = lax.psum_scatter(grad_rows, "net", scatter_dimension=0, tiled=True)
    own_float = unit_own.astype(jnp.float32)
    image_float = image_unit.astype(jnp.float32)
    own_totals = lax.dynamic_slice_in_dim(row_totals, net_index * rows_dev, rows_dev, 0)
    own_logit = logit_scale * jnp.sum(own_float * image_float, axis=1)
    pair_loss = jnp.log(own_totals) - own_logit
    return (
        pair_loss,
        row_total - logit_scale * image_float,
        column_total - logit_scale * own_float,
    )


def solution(mesh):
    in_specs = (
        P(("groups", "dp", "net"), None),
        P(("groups", "dp", "net")),
        P(("groups", "dp", "net"), None),
        P("groups", None),
    )
    out_specs = (
        P(("groups", "dp", "net")),
        P(("groups", "dp", "net"), None),
        P(("groups", "dp", "net"), None),
    )
    return jax.shard_map(
        per_device, mesh=mesh, in_specs=in_specs, out_specs=out_specs, check_vma=False
    )
```

profile of v0, /device:TPU:0, one launch (start us, length us, event | category | flops | bytes accessed | tf_op | source)
XLA Modules:
  0.0 143.5 jit_solution(11546669743643653315)
XLA Ops:
  8.1 1.3 fusion.15
  15.4 8.3 %all-reduce = f32[512]{0:T(512)S(1)} all-reduce(f32[512]{0:T(512)S(1)} %convert_reduce_fusion), channel_id=3, replica_groups=mesh['groups'=2,'dp'=4,'net'=4] {'net'}, use_global_device_ids=true, to_apply=%region_3.0.clone | all-reduce | flops 512 | bytes 4096
  24.0 14.2 %reduce-scatter.3.cloned.1.call-done = f32[128,512]{1,0:T(8,128)} async-done(((f32[512,512]{1,0:T(8,128)}), f32[128,512]{1,0:T(8,128)}) %reduce-scatter.3.cloned.1.call-update) | async-done | bytes 262160 | tf_op jit(solution)/shard_map/reduce_scatter | solution.py:44
  38.2 1.2 multiply_reduce_fusion
  39.5 6.8 %all_gather.6 = bf16[512,512]{1,0:T(8,128)(2,1)S(1)} all-gather(bf16[128,512]{1,0:T(8,128)(2,1)S(1)} %multiply_convert_fusion), channel_id=1, replica_groups=mesh['groups'=2,'dp'=4,'net'=4] {'net'}, dimensions={0}, use_global_device_ids=true | all-gather | bytes 655360 | tf_op jit(solution)/shard_map/all_gather | solution.py:47
  46.5 16.1 %all_gather.7 = bf16[512,512]{1,0:T(8,128)(2,1)S(1)} all-gather(bf16[128,512]{1,0:T(8,128)(2,1)S(1)} %get-tuple-element.428), channel_id=1, replica_groups=mesh['groups'=2,'dp'=4,'net'=4] {'dp'}, dimensions={0}, use_global_device_ids=true | all-gather | bytes 655360 | tf_op jit(solution)/shard_map/all_gather | solution.py:75
  62.6 0.9 conditional.3
  63.4 5.7 %psum.7 = f32[512]{0:T(512)S(1)} all-reduce(f32[512]{0:T(512)S(1)} %get-tuple-element.467), channel_id=1, replica_groups=mesh['groups'=2,'dp'=4,'net'=4] {'net'}, use_global_device_ids=true, to_apply=%region_9.10 | all-reduce | flops 512 | bytes 4096 | tf_op jit(solution)/shard_map/psum | solution.py:85
  69.2 41.1 %while.19 = (s32[]{:T(128)}, bf16[128,512]{1,0:T(8,128)(2,1)S(1)}, f32[128,512]{1,0:T(8,128)S(1)}, f32[512,512]{1,0:T(8,128)S(1)}, s32[]{:T(128)}, /*index=5*/f3...) while((s32[]{:T(128)}, bf16[128,512]{1,0:T(8,128)(2,1)S(1)}, ...), condition=%wide.region_16.17_spmd, body=%wide.region_12.16_spmd.sunk | while | flops 202244128 | bytes 6691314 | solution.py:123
  70.6 1.0 conditional.6
  71.6 1.8 %collective-permute-start.1 = (f32[128,512]{1,0:T(8,128)S(1)}, f32[128,512]{1,0:T(8,128)S(1)}, u32[]{:S(2)}, u32[]{:S(2)}) collective-permute-start(f32[128,512]{1,0:T(8,128)S(1)} %get-tuple-element.421), channel_id=1, source_target_pairs={{12,0},{0,4},{4,8},{8,12},{13,1},{1,5},{5,9},{9,13},{14,2},{2,6},{... | collective-permute-start | bytes 786440 | tf_op jit(solution)/shard_map/while/body/eval_jaxpr/ppermute | solution.py:15
  73.5 9.2 %collective-permute-done.1 = f32[128,512]{1,0:T(8,128)S(1)} collective-permute-done((f32[128,512]{1,0:T(8,128)S(1)}, f32[128,512]{1,0:T(8,128)S(1)}, u32[]{:S(2)}, u32[]{:S(2)}) %collective-permute-start.1) | collective-permute-done | bytes 262176 | tf_op jit(solution)/shard_map/while/body/eval_jaxpr/ppermute | solution.py:15
  82.6 1.9 %collective-permute-done = bf16[128,512]{1,0:T(8,128)(2,1)S(1)} collective-permute-done((bf16[128,512]{1,0:T(8,128)(2,1)S(1)}, bf16[128,512]{1,0:T(8,128)(2,1)S(1)}, u32[]{:S(2)}, u32[]{:S(2)}) %collective-permute-start) | collective-permute-done | bytes 131104 | tf_op jit(solution)/shard_map/while/body/eval_jaxpr/ppermute | solution.py:15
  85.9 1.3 collective-permute-start
  87.2 9.2 %collective-permute-done.1 = f32[128,512]{1,0:T(8,128)S(1)} collective-permute-done((f32[128,512]{1,0:T(8,128)S(1)}, f32[128,512]{1,0:T(8,128)S(1)}, u32[]{:S(2)}, u32[]{:S(2)}) %collective-permute-start.1) | collective-permute-done | bytes 262176 | tf_op jit(solution)/shard_map/while/body/eval_jaxpr/ppermute | solution.py:15
  96.5 1.4 collective-permute-done
  99.4 9.6 %collective-permute-done.1 = f32[128,512]{1,0:T(8,128)S(1)} collective-permute-done((f32[128,512]{1,0:T(8,128)S(1)}, f32[128,512]{1,0:T(8,128)S(1)}, u32[]{:S(2)}, u32[]{:S(2)}) %collective-permute-start.1) | collective-permute-done | bytes 262176 | tf_op jit(solution)/shard_map/while/body/eval_jaxpr/ppermute | solution.py:15
  109.0 1.4 collective-permute-done
  110.4 1.1 conditional.4
  111.5 1.0 copy-done.1
  113.1 7.6 %collective-permute-done.2 = f32[128,512]{1,0:T(8,128)S(1)} collective-permute-done((f32[128,512]{1,0:T(8,128)S(1)}, f32[128,512]{1,0:T(8,128)S(1)}, u32[]{:S(2)}, u32[]{:S(2)}) %collective-permute-start.2) | collective-permute-done | bytes 262176 | tf_op jit(solution)/shard_map/ppermute | solution.py:15
  120.7 0.7 fusion.18
  121.4 13.6 %reduce-scatter.5.cloned.1.call-done = f32[128,512]{1,0:T(8,128)} async-done(((f32[512,512]{1,0:T(8,128)}), f32[128,512]{1,0:T(8,128)}) %reduce-scatter.5.cloned.1.call-update) | async-done | bytes 262160 | tf_op jit(solution)/shard_map/reduce_scatter | solution.py:126
  135.0 1.7 %fusion.20 = f32[128,512]{1,0:T(8,128)} fusion(f32[128,512]{1,0:T(8,128)} %reduce-scatter.5.cloned.1.call-done, bf16[128,512]{1,0:T(8,128)(2,1)S(1)} %get-tuple-element.428), kind=kLoop, calls=%fused_computation.38 | loop fusion | flops 196608 | bytes 655360 | tf_op jit(solution)/shard_map/sub | solution.py:134
  (64 shorter events, 11.3 us)
Async XLA Ops:
  7.2 1.0 copy-start
  7.2 31.0 %reduce-scatter.3.cloned.1.call-start = ((), (), s32[]{:S(2)}) async-start(), calls=%async_computation.2 | async-start | bytes 1310720 | tf_op jit(solution)/shard_map/reduce_scatter | solution.py:44
  7.2 0.7 copy-start.4
  9.5 14.4 %copy-start.3 = (bf16[128,512]{1,0:T(8,128)(2,1)S(1)}, bf16[128,512]{1,0:T(8,128)(2,1)}, u32[]{:S(2)}) copy-start(bf16[128,512]{1,0:T(8,128)(2,1)} %param.14) | copy-start | bytes 393220
  9.5 125.6 %reduce-scatter.5.cloned.1.call-start = ((), (), s32[]{:S(2)}) async-start(), calls=%async_computation.3 | async-start | bytes 1310720 | tf_op jit(solution)/shard_map/reduce_scatter | solution.py:126
  13.4 0.7 copy-start.5
  38.2 1.2 copy-start.2
  71.6 11.0 %collective-permute-start.1 = (f32[128,512]{1,0:T(8,128)S(1)}, f32[128,512]{1,0:T(8,128)S(1)}, u32[]{:S(2)}, u32[]{:S(2)}) collective-permute-start(f32[128,512]{1,0:T(8,128)S(1)} %get-tuple-element.421), channel_id=1, source_target_pairs={{12,0},{0,4},{4,8},{8,12},{13,1},{1,5},{5,9},{9,13},{14,2},{2,6},{... | collective-permute-start | bytes 786440 | tf_op jit(solution)/shard_map/while/body/eval_jaxpr/ppermute | solution.py:15
  73.4 11.1 %collective-permute-start = (bf16[128,512]{1,0:T(8,128)(2,1)S(1)}, bf16[128,512]{1,0:T(8,128)(2,1)S(1)}, u32[]{:S(2)}, u32[]{:S(2)}) collective-permute-start(bf16[128,512]{1,0:T(8,128)(2,1)S(1)} %copy.32), channel_id=1, source_target_pairs={{12,0},{0,4},{4,8},{8,12},{13,1},{1,5},{5,9},{9,13},{14,2},{2,6},{... | collective-permute-start | bytes 393224 | tf_op jit(solution)/shard_map/while/body/eval_jaxpr/ppermute | solution.py:15
  85.8 10.7 %collective-permute-start.1 = (f32[128,512]{1,0:T(8,128)S(1)}, f32[128,512]{1,0:T(8,128)S(1)}, u32[]{:S(2)}, u32[]{:S(2)}) collective-permute-start(f32[128,512]{1,0:T(8,128)S(1)} %get-tuple-element.421), channel_id=1, source_target_pairs={{12,0},{0,4},{4,8},{8,12},{13,1},{1,5},{5,9},{9,13},{14,2},{2,6},{... | collective-permute-start | bytes 786440 | tf_op jit(solution)/shard_map/while/body/eval_jaxpr/ppermute | solution.py:15
  85.9 12.0 %collective-permute-start = (bf16[128,512]{1,0:T(8,128)(2,1)S(1)}, bf16[128,512]{1,0:T(8,128)(2,1)S(1)}, u32[]{:S(2)}, u32[]{:S(2)}) collective-permute-start(bf16[128,512]{1,0:T(8,128)(2,1)S(1)} %copy.32), channel_id=1, source_target_pairs={{12,0},{0,4},{4,8},{8,12},{13,1},{1,5},{5,9},{9,13},{14,2},{2,6},{... | collective-permute-start | bytes 393224 | tf_op jit(solution)/shard_map/while/body/eval_jaxpr/ppermute | solution.py:15
  99.2 9.7 %collective-permute-start.1 = (f32[128,512]{1,0:T(8,128)S(1)}, f32[128,512]{1,0:T(8,128)S(1)}, u32[]{:S(2)}, u32[]{:S(2)}) collective-permute-start(f32[128,512]{1,0:T(8,128)S(1)} %get-tuple-element.421), channel_id=1, source_target_pairs={{12,0},{0,4},{4,8},{8,12},{13,1},{1,5},{5,9},{9,13},{14,2},{2,6},{... | collective-permute-start | bytes 786440 | tf_op jit(solution)/shard_map/while/body/eval_jaxpr/ppermute | solution.py:15
  99.3 11.1 %collective-permute-start = (bf16[128,512]{1,0:T(8,128)(2,1)S(1)}, bf16[128,512]{1,0:T(8,128)(2,1)S(1)}, u32[]{:S(2)}, u32[]{:S(2)}) collective-permute-start(bf16[128,512]{1,0:T(8,128)(2,1)S(1)} %copy.32), channel_id=1, source_target_pairs={{12,0},{0,4},{4,8},{8,12},{13,1},{1,5},{5,9},{9,13},{14,2},{2,6},{... | collective-permute-start | bytes 393224 | tf_op jit(solution)/shard_map/while/body/eval_jaxpr/ppermute | solution.py:15
  111.5 1.0 copy-start.1
  112.5 8.2 %collective-permute-start.2 = (f32[128,512]{1,0:T(8,128)S(1)}, f32[128,512]{1,0:T(8,128)S(1)}, u32[]{:S(2)}, u32[]{:S(2)}) collective-permute-start(f32[128,512]{1,0:T(8,128)S(1)} %get-tuple-element.273), channel_id=1, source_target_pairs={{12,0},{0,4},{4,8},{8,12},{13,1},{1,5},{5,9},{9,13},{14,2},{2,6},{... | collective-permute-start | bytes 786440 | tf_op jit(solution)/shard_map/ppermute | solution.py:15
Sparse Core Ops, SparseCore 0:
  10.5 27.5 reduce-scatter.2
  112.6 22.3 reduce-scatter.4
where the time goes:
time: 145 us; the launch traced here: 144 us
  waiting for transfers between devices  68 us (47%)
  blocking collectives  36.9 us (25%)
  between operations  16.2 us (11%)
  other arithmetic  8.12 us (6%)
  local copies, waits for them, and re-layouts  5.04 us (3%)
  matrix products  3.61 us (2%)
  starting transfers between devices  3.52 us (2%)
  loops' own time  2.2 us (2%)
    ppermute x7, waiting for transfers between devices, passed_along(): return lax.ppermute(block, axis, route)  40.2 us
    all_gather x1, blocking collectives, per_device(): shard_rows = lax.all_gather(image_unit, 'dp', axis=0, tiled=True)  16.1 us
    reduce_scatter x1, waiting for transfers between devices, per_device(): lax.psum_scatter(partial_sums, 'net', scatter_dimension=0, tiled=True)  14.2 us
    reduce_scatter x1, waiting for transfers between devices, per_device(): lax.psum_scatter(grad_rows, 'net', scatter_dimension=0, tiled=True)  13.6 us
    unnamed x1, blocking collectives  8.34 us
    all_gather x1, blocking collectives, per_device(): lax.all_gather(unit_rows(pooled_sums / pooled_counts[:, None]), 'net', ax...  6.78 us
    psum x1, blocking collectives, per_device(): row_totals = lax.psum(partial_totals, 'net')  5.67 us
    ppermute x7, starting transfers between devices, passed_along(): return lax.ppermute(block, axis, route)  3.44 us
  transfers between devices with their start and end apart: 9, of which 9 were waited for; matrix products, arithmetic and copies ran while one was open for 3% of the time, Pallas kernels for 0%

commit v1 on v0

v1 whole, which is shorter than its diff:
```python
import functools

import jax
import jax.numpy as jnp
from jax import lax
from jax.experimental import pallas as pl
from jax.experimental.pallas import tpu as pltpu
from jax.sharding import PartitionSpec as P

BLOCK = 128
CHUNKS = 2
MESH = pl.DeviceIdType.MESH

logit_scale = 10.0


def each(count, body):
    if count <= 4:
        for k in range(1, count):
            body(k)
    else:

        def step(k, carry):
            body(k)
            return carry

        lax.fori_loop(1, count, step, 0)


def ordered_offset(k, size):
    if isinstance(k, int):
        return (k + 1) // 2 if k % 2 else size - k // 2
    return jnp.where(lax.rem(k, 2) == 1, lax.div(k + 1, 2), size - lax.div(k, 2))


def send(src, dst, send_sem, recv_sem, axis, peer):
    return pltpu.make_async_remote_copy(
        src_ref=src,
        dst_ref=dst,
        send_sem=send_sem,
        recv_sem=recv_sem,
        device_id={axis: peer},
        device_id_type=MESH,
    )


def kernel(
    net_size,
    dp_size,
    part_hbm,
    assign_ref,
    img_hbm,
    neg_ref,
    loss_ref,
    net_grad_ref,
    img_grad_ref,
    img_raw,
    part_all,
    assign_all,
    img_all,
    pooled,
    counted,
    unit,
    weights,
    soft,
    tot_all,
    total,
    row_out,
    row_in,
    col_out,
    col_in,
    local_sem,
    part_s,
    part_r,
    fwd_s,
    asg_s,
    asg_r,
    img_s,
    img_r,
    tot_s,
    tot_r,
    row_s,
    row_r,
    col_s,
    col_r,
):
    f32, bf16 = jnp.float32, jnp.bfloat16
    rows = img_raw.shape[0]
    part_rows = part_all.shape[1]
    chunk = part_rows // CHUNKS
    pair_dp = rows * net_size
    row_blocks = pair_dp // BLOCK
    own_blocks = rows // BLOCK
    chips = net_size // 2

    n = lax.axis_index("net")
    d = lax.axis_index("dp")
    core = lax.rem(n, 2)
    chip = lax.div(n, 2)
    sibling = n + 1 - 2 * core

    def net_peer(k):
        return lax.rem(n + k, net_size)

    def dp_peer(k):
        return lax.rem(d + k, dp_size)

    def chip_peer(k):
        return lax.rem(chip + k, chips)

    img_load = pltpu.make_async_copy(img_hbm, img_raw, local_sem.at[0])
    part_load = pltpu.make_async_copy(part_hbm, part_all.at[n], local_sem.at[1])
    img_load.start()
    part_load.start()

    barrier = pltpu.get_barrier_semaphore()
    each(
        net_size,
        lambda k: pl.semaphore_signal(
            barrier, inc=1, device_id={"net": net_peer(k)}, device_id_type=MESH
        ),
    )
    each(
        dp_size,
        lambda k: pl.semaphore_signal(
            barrier, inc=1, device_id={"dp": dp_peer(k)}, device_id_type=MESH
        ),
    )

    img_load.wait()
    h = img_raw[...].astype(f32)
    squares = jnp.sum(h * h, axis=1, keepdims=True)
    img_all[d] = (h * lax.rsqrt(squares + 1e-06)).astype(bf16)

    pl.semaphore_wait(barrier, net_size + dp_size - 2)

    def img_copy(k):
        off = ordered_offset(k, dp_size)
        return send(
            img_all.at[d], img_all.at[d], img_s.at[off], img_r.at[d], "dp", dp_peer(off)
        )

    def img_arrival(src):
        return send(img_all.at[src], img_all.at[src], img_s.at[0], img_r.at[src], "dp", d)

    def part_piece(ref, c):
        return ref.at[pl.ds(c * chunk, chunk)]

    def part_cross(k, c):
        return send(
            part_piece(part_hbm, c),
            part_piece(part_all.at[n], c),
            part_s.at[k, c],
            part_r.at[n, c],
            "net",
            chip_peer(k) * 2 + core,
        )

    def part_sibling(c):
        return send(
            part_piece(part_hbm, c),
            part_piece(part_all.at[n], c),
            part_s.at[0, c],
            part_r.at[n, c],
            "net",
            sibling,
        )

    def part_forward(k, c):
        origin = chip_peer(k) * 2 + core
        return send(
            part_piece(part_all.at[origin], c),
            part_piece(part_all.at[origin], c),
            fwd_s.at[k, c],
            part_r.at[origin, c],
            "net",
            sibling,
        )

    def part_arrival(origin, c):
        return send(
            part_piece(part_all.at[origin], c),
            part_piece(part_all.at[origin], c),
            part_s.at[0, c],
            part_r.at[origin, c],
            "net",
            sibling,
        )

    def asg_copy(k):
        return send(
            assign_ref, assign_all.at[n], asg_s.at[k], asg_r.at[n], "net", net_peer(k)
        )

    def asg_arrival(src):
        return send(
            assign_ref, assign_all.at[src], asg_s.at[0], asg_r.at[src], "net", sibling
        )

    each(net_size, lambda k: asg_copy(k).start())
    for c in range(CHUNKS):
        each(chips, lambda k: part_cross(k, c).start())
    each(dp_size, lambda k: img_copy(k).start())
    for c in range(CHUNKS):
        part_sibling(c).start()

    pair_ids = d * pair_dp + lax.broadcasted_iota(jnp.int32, (pair_dp, part_rows), 0)

    def pool(origin, assigned, first=False):
        member = (assigned == pair_ids).astype(f32)
        sums = jnp.dot(member.astype(bf16), part_all[origin], preferred_element_type=f32)
        counts = jnp.sum(member, axis=1, keepdims=True)
        if first:
            pooled[...] = sums
            counted[...] = counts
        else:
            pooled[...] += sums
            counted[...] += counts

    part_load.wait()
    pool(n, assign_ref[...], first=True)

    def pool_from(origin):
        asg_arrival(origin).wait_recv()
        pool(origin, assign_all[origin])

    for c in range(CHUNKS):
        part_arrival(sibling, c).wait_recv()
    pool_from(sibling)

    def pass_on(k):
        origin = chip_peer(k) * 2 + core
        for c in range(CHUNKS):
            part_arrival(origin, c).wait_recv()
            part_forward(k, c).start()
        pool_from(origin)

    each(chips, pass_on)

    def pool_passed(k):
        origin = chip_peer(k) * 2 + 1 - core
        for c in range(CHUNKS):
            part_arrival(origin, c).wait_recv()
        pool_from(origin)

    each(chips, pool_passed)

    p = pooled[...]
    cnt = counted[...]
    unit[...] = (
        p * lax.rsqrt(jnp.sum(p * p, axis=1, keepdims=True) + 1e-06 * (cnt * cnt))
    ).astype(bf16)

    def score(src):
        logits = logit_scale * lax.dot_general(
            img_all[src],
            unit[...],
            (((1,), (1,)), ((), ())),
            preferred_element_type=f32,
        )
        w = jnp.exp(logits)
        for q in range(own_blocks):
            column = (src * net_size + n) * own_blocks + q
            marks = []
            for b in range(row_blocks):
                row = d * row_blocks + b
                live = jnp.maximum(neg_ref[row, column], (row == column).astype(jnp.int32))
                marks.append(jnp.full((1, BLOCK), live.astype(f32), f32))
            masked = w[q * BLOCK : (q + 1) * BLOCK] * jnp.concatenate(marks, axis=1)
            start = pl.multiple_of(src * rows + q * BLOCK, BLOCK)
            weights[pl.ds(start, BLOCK), :] = masked
            tot_all[n] += jnp.sum(masked, axis=0, keepdims=True)

    tot_all[n] = jnp.zeros_like(tot_all[n])
    score(d)

    def score_from(k):
        src = dp_peer(ordered_offset(k, dp_size))
        img_arrival(src).wait_recv()
        score(src)

    each(dp_size, score_from)

    def tot_copy(k):
        return send(
            tot_all.at[n], tot_all.at[n], tot_s.at[k], tot_r.at[n], "net", net_peer(k)
        )

    def tot_arrival(src):
        return send(tot_all.at[src], tot_all.at[src], tot_s.at[0], tot_r.at[src], "net", sibling)

    each(net_size, lambda k: tot_copy(k).start())
    total[...] = tot_all[n]

    own = pl.ds(pl.multiple_of(n * rows, BLOCK), rows)
    own_logits = logit_scale * lax.dot_general(
        img_all[d], unit[own, :], (((1,), (1,)), ((), ())), preferred_element_type=f32
    )
    on_diagonal = lax.broadcasted_iota(jnp.int32, (rows, rows), 0) == lax.broadcasted_iota(
        jnp.int32, (rows, rows), 1
    )
    own_logit = jnp.sum(jnp.where(on_diagonal, own_logits, 0.0), axis=0, keepdims=True)

    def add_total(k):
        src = net_peer(k)
        tot_arrival(src).wait_recv()
        total[...] += tot_all[src]

    each(net_size, add_total)
    inverse = 1.0 / total[...]
    loss_ref[...] = jnp.log(total[:, own]) - own_logit

    def column_grad(src):
        span = pl.ds(pl.multiple_of(src * rows, BLOCK), rows)
        s = (weights[span, :] * inverse).astype(bf16)
        soft[span, :] = s
        return jnp.dot(s, unit[...], preferred_element_type=f32)

    def col_copy(k):
        off = ordered_offset(dp_size - k, dp_size)
        peer = dp_peer(off)
        return send(
            col_out.at[peer], col_in.at[d], col_s.at[off], col_r.at[d], "dp", peer
        )

    def col_arrival(src):
        return send(col_out.at[src], col_in.at[src], col_s.at[0], col_r.at[src], "dp", d)

    def column_send(k):
        peer = dp_peer(ordered_offset(dp_size - k, dp_size))
        col_out[peer] = column_grad(peer).astype(bf16)
        col_copy(k).start()

    each(dp_size, column_send)
    img_grad_ref[...] = column_grad(d) - unit[own, :].astype(f32)

    every_image = img_all[...].reshape(dp_size * rows, img_all.shape[2])

    def row_grad(dst):
        span = pl.ds(pl.multiple_of(dst * rows, BLOCK), rows)
        return lax.dot_general(
            soft[:, span], every_image, (((0,), (0,)), ((), ())), preferred_element_type=f32
        )

    def row_copy(k):
        peer = net_peer(k)
        return send(row_out.at[peer], row_in.at[n], row_s.at[k], row_r.at[n], "net", peer)

    def row_arrival(src):
        return send(row_out.at[src], row_in.at[src], row_s.at[0], row_r.at[src], "net", sibling)

    def row_send(k):
        peer = net_peer(k)
        row_out[peer] = row_grad(peer).astype(bf16)
        row_copy(k).start()

    each(net_size, row_send)
    net_grad_ref[...] = row_grad(n) - img_all[d].astype(f32)

    def row_add(k):
        src = net_peer(k)
        row_arrival(src).wait_recv()
        net_grad_ref[...] += row_in[src].astype(f32)

    each(net_size, row_add)
    net_grad_ref[...] = logit_scale * net_grad_ref[...]

    def col_add(k):
        src = dp_peer(ordered_offset(k, dp_size))
        col_arrival(src).wait_recv()
        img_grad_ref[...] += col_in[src].astype(f32)

    each(dp_size, col_add)
    img_grad_ref[...] = logit_scale * img_grad_ref[...]

    def net_done(k):
        asg_copy(k).wait_send()
        tot_copy(k).wait_send()
        row_copy(k).wait_send()

    def dp_done(k):
        img_copy(k).wait_send()
        col_copy(k).wait_send()

    each(net_size, net_done)
    each(dp_size, dp_done)
    for c in range(CHUNKS):
        part_sibling(c).wait_send()

        def chip_done(k):
            part_cross(k, c).wait_send()
            part_forward(k, c).wait_send()

        each(chips, chip_done)


def per_device(part_emb, assign, images, negatives):
    rows, width = images.shape
    part_rows = part_emb.shape[0]
    net_size = lax.axis_size("net")
    dp_size = lax.axis_size("dp")
    chips = net_size // 2
    pair_dp = rows * net_size
    columns = rows * dp_size
    f32, bf16 = jnp.float32, jnp.bfloat16
    dma = pltpu.SemaphoreType.DMA
    vmem = pl.BlockSpec(memory_space=pltpu.VMEM)
    smem = pl.BlockSpec(memory_space=pltpu.SMEM)
    hbm = pl.BlockSpec(memory_space=pl.ANY)
    loss, net_grad, img_grad = pl.pallas_call(
        functools.partial(kernel, net_size, dp_size),
        out_shape=(
            jax.ShapeDtypeStruct((1, rows), f32),
            jax.ShapeDtypeStruct((rows, width), f32),
            jax.ShapeDtypeStruct((rows, width), f32),
        ),
        in_specs=[hbm, vmem, hbm, smem],
        out_specs=(vmem, vmem, vmem),
        scratch_shapes=[
            pltpu.VMEM((rows, width), bf16),
            pltpu.VMEM((net_size, part_rows, width), bf16),
            pltpu.VMEM((net_size, 1, part_rows), jnp.int32),
            pltpu.VMEM((dp_size, rows, width), bf16),
            pltpu.VMEM((pair_dp, width), f32),
            pltpu.VMEM((pair_dp, 1), f32),
            pltpu.VMEM((pair_dp, width), bf16),
            pltpu.VMEM((columns, pair_dp), f32),
            pltpu.VMEM((columns, pair_dp), bf16),
            pltpu.VMEM((net_size, 1, pair_dp), f32),
            pltpu.VMEM((1, pair_dp), f32),
            pltpu.VMEM((net_size, rows, width), bf16),
            pltpu.VMEM((net_size, rows, width), bf16),
            pltpu.VMEM((dp_size, rows, width), bf16),
            pltpu.VMEM((dp_size, rows, width), bf16),
            dma((2,)),
            dma((chips, CHUNKS)),
            dma((net_size, CHUNKS)),
            dma((chips, CHUNKS)),
            dma((net_size,)),
            dma((net_size,)),
            dma((dp_size,)),
            dma((dp_size,)),
            dma((net_size,)),
            dma((net_size,)),
            dma((net_size,)),
            dma((net_size,)),
            dma((dp_size,)),
            dma((dp_size,)),
        ],
        compiler_params=pltpu.CompilerParams(
            collective_id=0, has_side_effects=True, vmem_limit_bytes=48 * 2**20
        ),
    )(part_emb, assign.reshape(1, part_rows), images, negatives)
    return loss.reshape(rows), net_grad, img_grad


def solution(mesh):
    in_specs = (
        P(("groups", "dp", "net"), None),
        P(("groups", "dp", "net")),
        P(("groups", "dp", "net"), None),
        P("groups", None),
    )
    out_specs = (
        P(("groups", "dp", "net")),
        P(("groups", "dp", "net"), None),
        P(("groups", "dp", "net"), None),
    )
    return jax.shard_map(
        per_device, mesh=mesh, in_specs=in_specs, out_specs=out_specs, check_vma=False
    )
```

time: 145 us -> 40.4 us (0.28)
  waiting for transfers between devices: 68 us -> 0 us
  blocking collectives: 36.9 us -> 0 us
  Pallas kernels: 0 us -> 34.4 us
  between operations: 16.2 us -> 0.65 us
  other arithmetic: 8.12 us -> 0 us
  matrix products: 3.61 us -> 0 us
  starting transfers between devices: 3.52 us -> 0 us
  loops' own time: 2.2 us -> 0 us
    ppermute x7 -> x0, waiting for transfers between devices: 40.2 us -> none  [passed_along(): return lax.ppermute(block, axis, route)]
    pallas_call x0 -> x1, Pallas kernels: none -> 34.4 us  [per_device(): pl.pallas_call(functools.partial(kernel, net_size, dp_size), out_shape=(j...]
    reduce_scatter x2 -> x0, waiting for transfers between devices: 27.8 us -> none  [the longest x1 14.2 us: per_device(): lax.psum_scatter(partial_sums, 'net', scatter_dimension=0, tiled=True)]
    all_gather x2 -> x0, blocking collectives: 22.9 us -> none  [the longest x1 16.1 us: per_device(): shard_rows = lax.all_gather(image_unit, 'dp', axis=0, tiled=True)]
    unnamed x1 -> x0, blocking collectives: 8.34 us -> none
    psum x1 -> x0, blocking collectives: 5.67 us -> none  [per_device(): row_totals = lax.psum(partial_totals, 'net')]
    dot_general x8 -> x0, matrix products: 3.61 us -> none  [the longest x1 1.31 us: per_device(): jnp.dot(member.astype(jnp.bfloat16), part_emb, preferred_element_type=jnp...]
    ppermute x7 -> x0, starting transfers between devices: 3.44 us -> none  [passed_along(): return lax.ppermute(block, axis, route)]
  transfers between devices with their start and end apart: 9 -> 0, of which waited for: 9 -> 0; matrix products, arithmetic and copies ran while one was open for 3% -> 0% of each run, Pallas kernels for 0% -> 0%
where the time goes in v1:
time: 40.4 us; the launch traced here: 40.2 us
  Pallas kernels  34.4 us (85%)
  local copies, waits for them, and re-layouts  5.14 us (13%)
  between operations  0.65 us (2%)
    pallas_call x1, Pallas kernels, per_device(): pl.pallas_call(functools.partial(kernel, net_size, dp_size), out_shape=(j...  34.4 us
    unnamed x11, local copies, waits for them, and re-layouts  5.14 us

profile of v1, /device:TPU:0, one launch (start us, length us, event | category | flops | bytes accessed | tf_op | source)
XLA Modules:
  0.0 40.2 jit_solution(15979756139983607368)
XLA Ops:
  0.6 0.0 copy-start.3
  0.6 0.7 %copy-done.3 = s32[256]{0:T(256)S(1)} copy-done((s32[256]{0:T(256)S(1)}, s32[256]{0:T(256)}, u32[]{:S(2)}) %copy-start.3) | copy-done | bytes 1048
  1.3 0.0 copy-start
  1.3 0.9 %copy-done = bf16[256,512]{1,0:T(8,128)(2,1)S(1)} copy-done((bf16[256,512]{1,0:T(8,128)(2,1)S(1)}, bf16[256,512]{1,0:T(8,128)(2,1)}, u32[]{:S(2)}) %copy-start) | copy-done | bytes 262168
  2.3 0.0 copy-start.1
  2.3 0.9 %copy-done.1 = bf16[128,512]{1,0:T(8,128)(2,1)S(1)} copy-done((bf16[128,512]{1,0:T(8,128)(2,1)S(1)}, bf16[128,512]{1,0:T(8,128)(2,1)}, u32[]{:S(2)}) %copy-start.1) | copy-done | bytes 131096
  3.2 0.0 copy-start.2
  3.2 0.7 %copy-done.2 = s32[16,16]{1,0:T(8,128)S(1)} copy-done((s32[16,16]{1,0:T(8,128)S(1)}, s32[16,16]{1,0:T(8,128)}, u32[]{:S(2)}) %copy-start.2) | copy-done | bytes 1048
  3.9 34.4 %shard_map.67 = (f32[1,128]{1,0:T(1,128)S(1)}, f32[128,512]{1,0:T(8,128)S(1)}, f32[128,512]{1,0:T(8,128)S(1)}) custom-call(bf16[256,512]{1,0:T(8,128)(2,1)S(1)} %copy-done, s32[1,256]{1,0:T(1,128)S(1)} %bitcast.2, bf16[128,512]{1,0:T(8,128)(2,1)S(1)} %copy-done.1, s32[16,16]{1,0:T(8,128)S(1)} %copy-done.2), custom_call_target="tpu_custom_call" | custom-call | tf_op jit(solution)/shard_map/pallas_call | solution.py:410
  38.2 0.5 %copy.10 = f32[128]{0:T(128)} copy(f32[128]{0:T(128)S(1)} %bitcast.3) | data formatting | bytes 1024
  38.8 0.7 %copy.11 = f32[128,512]{1,0:T(8,128)} copy(f32[128,512]{1,0:T(8,128)S(1)} %get-tuple-element.13) | data formatting | bytes 524288
  39.5 0.7 %copy.12 = f32[128,512]{1,0:T(8,128)} copy(f32[128,512]{1,0:T(8,128)S(1)} %get-tuple-element.14) | data formatting | bytes 524288
Async XLA Ops:
  0.6 0.7 %copy-start.3 = (s32[256]{0:T(256)S(1)}, s32[256]{0:T(256)}, u32[]{:S(2)}) copy-start(s32[256]{0:T(256)} %param.5) | copy-start | bytes 3076
  1.3 0.9 %copy-start = (bf16[256,512]{1,0:T(8,128)(2,1)S(1)}, bf16[256,512]{1,0:T(8,128)(2,1)}, u32[]{:S(2)}) copy-start(bf16[256,512]{1,0:T(8,128)(2,1)} %part_hbm.1) | copy-start | bytes 786436
  2.3 0.9 %copy-start.1 = (bf16[128,512]{1,0:T(8,128)(2,1)S(1)}, bf16[128,512]{1,0:T(8,128)(2,1)}, u32[]{:S(2)}) copy-start(bf16[128,512]{1,0:T(8,128)(2,1)} %img_hbm.1) | copy-start | bytes 393220
  3.2 0.7 %copy-start.2 = (s32[16,16]{1,0:T(8,128)S(1)}, s32[16,16]{1,0:T(8,128)}, u32[]{:S(2)}) copy-start(s32[16,16]{1,0:T(8,128)} %neg_ref.1) | copy-start | bytes 3076

commit v2 on v1

--- a/solution.py
+++ b/solution.py
@@ -27,10 +27,13 @@
         lax.fori_loop(1, count, step, 0)
 
 
-def ordered_offset(k, size):
-    if isinstance(k, int):
-        return (k + 1) // 2 if k % 2 else size - k // 2
-    return jnp.where(lax.rem(k, 2) == 1, lax.div(k + 1, 2), size - lax.div(k, 2))
+def line_peer(k, d, size):
+    surplus = jnp.maximum(size - 1 - 2 * d, 2 * d - size + 1)
+    reach = jnp.minimum(d, size - 1 - d)
+    far = jnp.where(2 * d < size - 1, size - 1 - k, k)
+    pair = jnp.maximum(k - surplus, 0)
+    near = d + (1 - 2 * lax.rem(pair, 2)) * (reach - lax.div(pair, 2))
+    return jnp.where(k < surplus, far, near)
 
 
 def send(src, dst, send_sem, recv_sem, axis, peer):
@@ -48,13 +51,14 @@
     net_size,
     dp_size,
     part_hbm,
-    assign_ref,
+    assign_hbm,
     img_hbm,
-    neg_ref,
+    neg_hbm,
     loss_ref,
     net_grad_ref,
     img_grad_ref,
     img_raw,
+    neg_ref,
     part_all,
     assign_all,
     img_all,
@@ -103,15 +107,15 @@
         return lax.rem(n + k, net_size)
 
     def dp_peer(k):
-        return lax.rem(d + k, dp_size)
+        return line_peer(k - 1, d, dp_size)
 
     def chip_peer(k):
         return lax.rem(chip + k, chips)
 
     img_load = pltpu.make_async_copy(img_hbm, img_raw, local_sem.at[0])
     part_load = pltpu.make_async_copy(part_hbm, part_all.at[n], local_sem.at[1])
-    img_load.start()
-    part_load.start()
+    asg_load = pltpu.make_async_copy(assign_hbm, assign_all.at[n], local_sem.at[2])
+    neg_load = pltpu.make_async_copy(neg_hbm, neg_ref, local_sem.at[3])
 
     barrier = pltpu.get_barrier_semaphore()
     each(
@@ -127,6 +131,10 @@
         ),
     )
 
+    img_load.start()
+    part_load.start()
+    asg_load.start()
+    neg_load.start()
     img_load.wait()
     h = img_raw[...].astype(f32)
     squares = jnp.sum(h * h, axis=1, keepdims=True)
@@ -135,9 +143,8 @@
     pl.semaphore_wait(barrier, net_size + dp_size - 2)
 
     def img_copy(k):
-        off = ordered_offset(k, dp_size)
-        return send(
-            img_all.at[d], img_all.at[d], img_s.at[off], img_r.at[d], "dp", dp_peer(off)
+        return send(
+            img_all.at[d], img_all.at[d], img_s.at[k], img_r.at[d], "dp", dp_peer(k)
         )
 
     def img_arrival(src):
@@ -189,12 +196,12 @@
 
     def asg_copy(k):
         return send(
-            assign_ref, assign_all.at[n], asg_s.at[k], asg_r.at[n], "net", net_peer(k)
+            assign_hbm, assign_all.at[n], asg_s.at[k], asg_r.at[n], "net", net_peer(k)
         )
 
     def asg_arrival(src):
         return send(
-            assign_ref, assign_all.at[src], asg_s.at[0], asg_r.at[src], "net", sibling
+            assign_hbm, assign_all.at[src], asg_s.at[0], asg_r.at[src], "net", sibling
         )
 
     each(net_size, lambda k: asg_copy(k).start())
@@ -218,7 +225,8 @@
             counted[...] += counts
 
     part_load.wait()
-    pool(n, assign_ref[...], first=True)
+    asg_load.wait()
+    pool(n, assign_all[n], first=True)
 
     def pool_from(origin):
         asg_arrival(origin).wait_recv()
@@ -271,11 +279,12 @@
             weights[pl.ds(start, BLOCK), :] = masked
             tot_all[n] += jnp.sum(masked, axis=0, keepdims=True)
 
+    neg_load.wait()
     tot_all[n] = jnp.zeros_like(tot_all[n])
     score(d)
 
     def score_from(k):
-        src = dp_peer(ordered_offset(k, dp_size))
+        src = dp_peer(dp_size - k)
         img_arrival(src).wait_recv()
         score(src)
 
@@ -317,17 +326,16 @@
         return jnp.dot(s, unit[...], preferred_element_type=f32)
 
     def col_copy(k):
-        off = ordered_offset(dp_size - k, dp_size)
-        peer = dp_peer(off)
-        return send(
-            col_out.at[peer], col_in.at[d], col_s.at[off], col_r.at[d], "dp", peer
+        peer = dp_peer(k)
+        return send(
+            col_out.at[peer], col_in.at[d], col_s.at[k], col_r.at[d], "dp", peer
         )
 
     def col_arrival(src):
         return send(col_out.at[src], col_in.at[src], col_s.at[0], col_r.at[src], "dp", d)
 
     def column_send(k):
-        peer = dp_peer(ordered_offset(dp_size - k, dp_size))
+        peer = dp_peer(k)
         col_out[peer] = column_grad(peer).astype(bf16)
         col_copy(k).start()
 
@@ -366,7 +374,7 @@
     net_grad_ref[...] = logit_scale * net_grad_ref[...]
 
     def col_add(k):
-        src = dp_peer(ordered_offset(k, dp_size))
+        src = dp_peer(dp_size - k)
         col_arrival(src).wait_recv()
         img_grad_ref[...] += col_in[src].astype(f32)
 
@@ -392,6 +400,19 @@
             part_forward(k, c).wait_send()
 
         each(chips, chip_done)
+
+
+def hand_over(loss, net_grad, img_grad, loss_out, net_out, img_out, sem):
+    copies = [
+        pltpu.make_async_copy(src, dst, sem.at[i])
+        for i, (src, dst) in enumerate(
+            ((loss, loss_out), (net_grad, net_out), (img_grad, img_out))
+        )
+    ]
+    for copy in copies:
+        copy.start()
+    for copy in copies:
+        copy.wait()
 
 
 def per_device(part_emb, assign, images, negatives):
@@ -405,19 +426,20 @@
     f32, bf16 = jnp.float32, jnp.bfloat16
     dma = pltpu.SemaphoreType.DMA
     vmem = pl.BlockSpec(memory_space=pltpu.VMEM)
-    smem = pl.BlockSpec(memory_space=pltpu.SMEM)
-    hbm = pl.BlockSpec(memory_space=pl.ANY)
+    hbm = pl.BlockSpec(memory_space=pltpu.HBM)
+    results = (
+        jax.ShapeDtypeStruct((1, rows), f32),
+        jax.ShapeDtypeStruct((rows, width), f32),
+        jax.ShapeDtypeStruct((rows, width), f32),
+    )
     loss, net_grad, img_grad = pl.pallas_call(
         functools.partial(kernel, net_size, dp_size),
-        out_shape=(
-            jax.ShapeDtypeStruct((1, rows), f32),
-            jax.ShapeDtypeStruct((rows, width), f32),
-            jax.ShapeDtypeStruct((rows, width), f32),
-        ),
-        in_specs=[hbm, vmem, hbm, smem],
+        out_shape=results,
+        in_specs=[hbm, hbm, hbm, hbm],
         out_specs=(vmem, vmem, vmem),
         scratch_shapes=[
             pltpu.VMEM((rows, width), bf16),
+            pltpu.SMEM(negatives.shape, jnp.int32),
             pltpu.VMEM((net_size, part_rows, width), bf16),
             pltpu.VMEM((net_size, 1, part_rows), jnp.int32),
             pltpu.VMEM((dp_size, rows, width), bf16),
@@ -432,7 +454,7 @@
             pltpu.VMEM((net_size, rows, width), bf16),
             pltpu.VMEM((dp_size, rows, width), bf16),
             pltpu.VMEM((dp_size, rows, width), bf16),
-            dma((2,)),
+            dma((4,)),
             dma((chips, CHUNKS)),
             dma((net_size, CHUNKS)),
             dma((chips, CHUNKS)),
@@ -450,7 +472,20 @@
         compiler_params=pltpu.CompilerParams(
             collective_id=0, has_side_effects=True, vmem_limit_bytes=48 * 2**20
         ),
-    )(part_emb, assign.reshape(1, part_rows), images, negatives)
+    )(*(
+        pltpu.with_memory_space_constraint(array, pltpu.HBM)
+        for array in (part_emb, assign.reshape(1, part_rows), images, negatives)
+    ))
+    loss, net_grad, img_grad = pl.pallas_call(
+        hand_over,
+        out_shape=results,
+        in_specs=[vmem] * 3,
+        out_specs=(hbm, hbm, hbm),
+        scratch_shapes=[dma((3,))],
+    )(*(
+        pltpu.with_memory_space_constraint(array, pltpu.VMEM)
+        for array in (loss, net_grad, img_grad)
+    ))
     return loss.reshape(rows), net_grad, img_grad
 
 

time: 40.4 us -> 34.2 us (0.85)
  local copies, waits for them, and re-layouts: 5.14 us -> 0 us
  Pallas kernels: 34.4 us -> 32.9 us
    unnamed x11 -> x0, local copies, waits for them, and re-layouts: 5.14 us -> none
    pallas_call x1 -> x2, Pallas kernels: 34.4 us -> 32.9 us  [the longest x1 32.1 us: per_device(): pl.pallas_call(functools.partial(kernel, net_size, dp_size), out_shape=re...]
where the time goes in v2:
time: 34.2 us; the launch traced here: 33.6 us
  Pallas kernels  32.9 us (96%)
  between operations  0.64 us (2%)
    pallas_call x1, Pallas kernels, per_device(): pl.pallas_call(functools.partial(kernel, net_size, dp_size), out_shape=re...  32.1 us
    pallas_call x1, Pallas kernels, per_device(): pl.pallas_call(hand_over, out_shape=results, in_specs=[vmem] * 3, out_spe...  0.82 us

profile of v2, /device:TPU:0, one launch (start us, length us, event | category | flops | bytes accessed | tf_op | source)
XLA Modules:
  0.0 33.6 jit_solution(6470163328908732531)
XLA Ops:
  0.6 32.1 %shard_map.67 = (f32[1,128]{1,0:T(1,128)S(1)}, f32[128,512]{1,0:T(8,128)S(1)}, f32[128,512]{1,0:T(8,128)S(1)}) custom-call(bf16[256,512]{1,0:T(8,128)(2,1)} %part_hbm.1, s32[1,256]{1,0:T(1,128)} %bitcast.2, bf16[128,512]{1,0:T(8,128)(2,1)} %img_hbm.1, s32[16,16]{1,0:T(8,128)} %neg_hbm.1), custom_call_target="tpu_custom_call" | custom-call | tf_op jit(solution)/shard_map/pallas_call | solution.py:435
  32.7 0.8 %shard_map.68 = (f32[1,128]{1,0:T(1,128)}, f32[128,512]{1,0:T(8,128)}, f32[128,512]{1,0:T(8,128)}) custom-call(f32[1,128]{1,0:T(1,128)S(1)} %get-tuple-element.9.loss, f32[128,512]{1,0:T(8,128)S(1)} %get-tuple-element.10.net_grad, f32[128,512]{1,0:T(8,128)S(1)} %get-tuple-element.11.img_grad), custom_call_target="tpu_custom_call" | custom-call | tf_op jit(solution)/shard_map/pallas_call | solution.py:479

commit v3 on v2

--- a/solution.py
+++ b/solution.py
@@ -87,6 +87,10 @@
     row_r,
     col_s,
     col_r,
+    held,
+    relay_in,
+    relay_s,
+    relay_r,
 ):
     f32, bf16 = jnp.float32, jnp.bfloat16
     rows = img_raw.shape[0]
@@ -147,6 +151,22 @@
             img_all.at[d], img_all.at[d], img_s.at[k], img_r.at[d], "dp", dp_peer(k)
         )
 
+    line = dp_size == 4
+    at_end = lax.rem(d, 3) == 0
+    in_middle = lax.rem(d, 3) > 0
+
+    def img_start(k):
+        if line and k == 1:
+            pl.when(in_middle)(lambda: img_copy(k).start())
+        else:
+            img_copy(k).start()
+
+    def img_relay():
+        src = dp_peer(1)
+        return send(
+            img_all.at[src], img_all.at[src], relay_s, img_r.at[src], "dp", 3 * d - 3
+        )
+
     def img_arrival(src):
         return send(img_all.at[src], img_all.at[src], img_s.at[0], img_r.at[src], "dp", d)
 
@@ -207,7 +227,7 @@
     each(net_size, lambda k: asg_copy(k).start())
     for c in range(CHUNKS):
         each(chips, lambda k: part_cross(k, c).start())
-    each(dp_size, lambda k: img_copy(k).start())
+    each(dp_size, img_start)
     for c in range(CHUNKS):
         part_sibling(c).start()
 
@@ -242,6 +262,13 @@
             part_arrival(origin, c).wait_recv()
             part_forward(k, c).start()
         pool_from(origin)
+
+    if line:
+
+        @pl.when(in_middle)
+        def _():
+            img_arrival(dp_peer(1)).wait_recv()
+            img_relay().start()
 
     each(chips, pass_on)
 
@@ -285,7 +312,10 @@
 
     def score_from(k):
         src = dp_peer(dp_size - k)
-        img_arrival(src).wait_recv()
+        if line and k == dp_size - 1:
+            pl.when(at_end)(lambda: img_arrival(src).wait_recv())
+        else:
+            img_arrival(src).wait_recv()
         score(src)
 
     each(dp_size, score_from)
@@ -334,10 +364,28 @@
     def col_arrival(src):
         return send(col_out.at[src], col_in.at[src], col_s.at[0], col_r.at[src], "dp", d)
 
+    def col_relay():
+        return send(
+            col_out.at[dp_peer(1)], relay_in, col_s.at[1], relay_r, "dp", dp_peer(dp_size - 1)
+        )
+
     def column_send(k):
         peer = dp_peer(k)
-        col_out[peer] = column_grad(peer).astype(bf16)
-        col_copy(k).start()
+        sums = column_grad(peer)
+        if line and k == 1:
+
+            @pl.when(at_end)
+            def _():
+                col_out[peer] = sums.astype(bf16)
+                col_relay().start()
+
+            @pl.when(in_middle)
+            def _():
+                held[...] = sums
+
+        else:
+            col_out[peer] = sums.astype(bf16)
+            col_copy(k).start()
 
     each(dp_size, column_send)
     img_grad_ref[...] = column_grad(d) - unit[own, :].astype(f32)
@@ -365,6 +413,15 @@
     each(net_size, row_send)
     net_grad_ref[...] = row_grad(n) - img_all[d].astype(f32)
 
+    if line:
+
+        @pl.when(in_middle)
+        def _():
+            col_relay().wait_recv()
+            far = dp_peer(1)
+            col_out[far] = (held[...] + relay_in[...].astype(f32)).astype(bf16)
+            col_copy(1).start()
+
     def row_add(k):
         src = net_peer(k)
         row_arrival(src).wait_recv()
@@ -375,8 +432,15 @@
 
     def col_add(k):
         src = dp_peer(dp_size - k)
-        col_arrival(src).wait_recv()
-        img_grad_ref[...] += col_in[src].astype(f32)
+
+        def add():
+            col_arrival(src).wait_recv()
+            img_grad_ref[...] += col_in[src].astype(f32)
+
+        if line and k == dp_size - 1:
+            pl.when(in_middle)(add)
+        else:
+            add()
 
     each(dp_size, col_add)
     img_grad_ref[...] = logit_scale * img_grad_ref[...]
@@ -387,8 +451,21 @@
         row_copy(k).wait_send()
 
     def dp_done(k):
-        img_copy(k).wait_send()
-        col_copy(k).wait_send()
+        if line and k == 1:
+
+            @pl.when(in_middle)
+            def _():
+                img_copy(k).wait_send()
+                img_relay().wait_send()
+
+            @pl.when(at_end)
+            def _():
+                col_relay().wait_send()
+
+            pl.when(in_middle)(lambda: col_copy(k).wait_send())
+        else:
+            img_copy(k).wait_send()
+            col_copy(k).wait_send()
 
     each(net_size, net_done)
     each(dp_size, dp_done)
@@ -468,6 +545,10 @@
             dma((net_size,)),
             dma((dp_size,)),
             dma((dp_size,)),
+            pltpu.VMEM((rows, width), f32),
+            pltpu.VMEM((rows, width), bf16),
+            dma(()),
+            dma(()),
         ],
         compiler_params=pltpu.CompilerParams(
             collective_id=0, has_side_effects=True, vmem_limit_bytes=48 * 2**20

time: 34.2 us -> 32.5 us (0.950); the launches traced: 33.6 us -> 32.3 us
  Pallas kernels: 32.9 us -> 31.7 us
    pallas_call x1, Pallas kernels: 32.1 us -> 30.9 us  [per_device(): pl.pallas_call(functools.partial(kernel, net_size, dp_size), out_shape=re...]
where the time goes in v3:
time: 32.5 us; the launch traced here: 32.3 us
  Pallas kernels  31.7 us (98%)
  between operations  0.64 us (2%)
    pallas_call x1, Pallas kernels, per_device(): pl.pallas_call(functools.partial(kernel, net_size, dp_size), out_shape=re...  30.9 us
    pallas_call x1, Pallas kernels, per_device(): pl.pallas_call(hand_over, out_shape=results, in_specs=[vmem] * 3, out_spe...  0.82 us

profile of v3, /device:TPU:0, one launch (start us, length us, event | category | flops | bytes accessed | tf_op | source)
XLA Modules:
  0.0 32.3 jit_solution(2729774236840454550)
XLA Ops:
  0.6 30.9 %shard_map.67 = (f32[1,128]{1,0:T(1,128)S(1)}, f32[128,512]{1,0:T(8,128)S(1)}, f32[128,512]{1,0:T(8,128)S(1)}) custom-call(bf16[256,512]{1,0:T(8,128)(2,1)} %part_hbm.1, s32[1,256]{1,0:T(1,128)} %bitcast.2, bf16[128,512]{1,0:T(8,128)(2,1)} %img_hbm.1, s32[16,16]{1,0:T(8,128)} %neg_hbm.1), custom_call_target="tpu_custom_call" | custom-call | tf_op jit(solution)/shard_map/pallas_call | solution.py:512
  31.5 0.8 %shard_map.68 = (f32[1,128]{1,0:T(1,128)}, f32[128,512]{1,0:T(8,128)}, f32[128,512]{1,0:T(8,128)}) custom-call(f32[1,128]{1,0:T(1,128)S(1)} %get-tuple-element.9.loss, f32[128,512]{1,0:T(8,128)S(1)} %get-tuple-element.10.net_grad, f32[128,512]{1,0:T(8,128)S(1)} %get-tuple-element.11.img_grad), custom_call_target="tpu_custom_call" | custom-call | tf_op jit(solution)/shard_map/pallas_call | solution.py:560

commit v4 on v3

--- a/solution.py
+++ b/solution.py
@@ -385,6 +385,8 @@
 
         else:
             col_out[peer] = sums.astype(bf16)
+            if line and k == 2:
+                pl.when(at_end)(lambda: col_relay().wait_send())
             col_copy(k).start()
 
     each(dp_size, column_send)
@@ -457,10 +459,6 @@
             def _():
                 img_copy(k).wait_send()
                 img_relay().wait_send()
-
-            @pl.when(at_end)
-            def _():
-                col_relay().wait_send()
 
             pl.when(in_middle)(lambda: col_copy(k).wait_send())
         else:

time: 32.5 us -> 32.5 us (level)
  no operation moved by 1% of the time
where the time goes in v4:
time: 32.5 us; the launch traced here: 32.3 us
  Pallas kernels  31.7 us (98%)
  between operations  0.64 us (2%)
    pallas_call x1, Pallas kernels, per_device(): pl.pallas_call(functools.partial(kernel, net_size, dp_size), out_shape=re...  30.9 us
    pallas_call x1, Pallas kernels, per_device(): pl.pallas_call(hand_over, out_shape=results, in_specs=[vmem] * 3, out_spe...  0.82 us

profile of v4, /device:TPU:0, one launch (start us, length us, event | category | flops | bytes accessed | tf_op | source)
XLA Modules:
  0.0 32.3 jit_solution(9805480208168497984)
XLA Ops:
  0.6 30.9 %shard_map.67 = (f32[1,128]{1,0:T(1,128)S(1)}, f32[128,512]{1,0:T(8,128)S(1)}, f32[128,512]{1,0:T(8,128)S(1)}) custom-call(bf16[256,512]{1,0:T(8,128)(2,1)} %part_hbm.1, s32[1,256]{1,0:T(1,128)} %bitcast.2, bf16[128,512]{1,0:T(8,128)(2,1)} %img_hbm.1, s32[16,16]{1,0:T(8,128)} %neg_hbm.1), custom_call_target="tpu_custom_call" | custom-call | tf_op jit(solution)/shard_map/pallas_call | solution.py:510
  31.5 0.8 %shard_map.68 = (f32[1,128]{1,0:T(1,128)}, f32[128,512]{1,0:T(8,128)}, f32[128,512]{1,0:T(8,128)}) custom-call(f32[1,128]{1,0:T(1,128)S(1)} %get-tuple-element.9.loss, f32[128,512]{1,0:T(8,128)S(1)} %get-tuple-element.10.net_grad, f32[128,512]{1,0:T(8,128)S(1)} %get-tuple-element.11.img_grad), custom_call_target="tpu_custom_call" | custom-call | tf_op jit(solution)/shard_map/pallas_call | solution.py:558
